TPU v7x, 256 devices: a whole 4x4x8 slice. The times are simulated.
256 devices in a mesh: batch: 16 (over x, y_hi, core), seq: 16 (over z, y_lo).
Axes of the slice: x: 4, y: 4 (y_hi: 2, y_lo: 2; y = y_hi * 2 + y_lo), z: 8, core: 2. Of those that a mesh axis runs over, the one named last changes fastest.
Arguments:
- dna_features: bfloat16 [131072, 768], P(('batch', 'seq')), parts along dimension 0, may hold values from -6 to 6
- conv_weight: bfloat16 [5, 768, 1536], P(None, None, 'seq'), may hold values from -0.09375 to 0.09375
- conv_bias: float32 [1536], replicated, may hold values from -3 to 3
- norm_gain: float32 [1536], replicated, may hold values from 0.5 to 1.5
- qkv_weight: bfloat16 [3, 1536, 768], P(None, None, 'seq'), may hold values from -0.15625 to 0.15625
- head_scale: float32 [4], replicated, may hold values from 1.5 to 60, as said below
- out_weight: bfloat16 [768, 1536], P(None, 'seq'), may hold values from -0.21875 to 0.21875
Outputs:
- block_out: bfloat16 [65536, 1536], P(('batch', 'seq')), parts along dimension 0
There are 16 independent parts, one for each index of `batch`. A program takes and returns all parts, laid end to end along the dimension named above; an argument that names none is the same for every part. Nothing has to cross between parts.
Inputs may be any that keep to these rules, and one draw needn't show every extreme that they name: `head_scale`: one positive factor per head.
All inputs are finite; a program needn't handle non-finite values.
Results may differ from a plain program's by a relative error of at most 0.017.
The roundings to bfloat16 on the way count: a program that leaves them out, or rounds other values in their place, can miss the bound.
Values may be sent and summed in bfloat16 or wider, within the bound.
No kernel may reach another device: no remote copies, remote signals or barrier semaphores. Data moves between devices by JAX's collectives and lax.ppermute only.
A program may use at most 128 MiB of HBM per device.

v0:
```python
import math
import jax
import jax.numpy as jnp
from jax import lax
from jax.sharding import PartitionSpec as P

HEADS = 4
HEAD_DIM = 192


def extended(block, sides, width):
    for axis, dim in sides:
        count = lax.axis_size(axis)
        forward = [(i, i + 1) for i in range(count - 1)]
        backward = [(target, source) for source, target in forward]
        low = lax.ppermute(
            lax.slice_in_dim(block, block.shape[dim] - width, None, axis=dim), axis, forward
        )
        high = lax.ppermute(lax.slice_in_dim(block, 0, width, axis=dim), axis, backward)
        block = jnp.concatenate([low, block, high], axis=dim)
    return block


def conv_whole(padded, kernel, bias_cols, positions):
    col_count = kernel.shape[2]
    summed = jnp.zeros((positions, col_count), jnp.float32) + bias_cols
    for tap in range(kernel.shape[0]):
        summed = summed + jnp.dot(
            padded[tap : tap + positions], kernel[tap], preferred_element_type=jnp.float32
        )
    return jnp.max(summed.reshape(positions // 2, 2, col_count), axis=1).astype(jnp.bfloat16)


def shards(dna_features, conv_weight, conv_bias, norm_gain, qkv_weight, head_scale, out_weight):
    tap_count = conv_weight.shape[0]
    half_taps = tap_count // 2
    activated = jax.nn.gelu(dna_features.astype(jnp.float32), approximate=True).astype(jnp.bfloat16)
    positions = activated.shape[0]
    padded = extended(activated, (("seq", 0),), half_taps)
    pooled = conv_whole(
        padded, lax.all_gather(conv_weight, "seq", axis=2, tiled=True), conv_bias, positions
    )
    tok_count = pooled.shape[0]
    values32 = pooled.astype(jnp.float32)
    centre = jnp.mean(values32, axis=1, keepdims=True)
    spread = jnp.mean((values32 - centre) ** 2, axis=1, keepdims=True)
    normed = ((values32 - centre) * lax.rsqrt(spread + 1e-05) * norm_gain).astype(jnp.bfloat16)
    projected = jnp.einsum(
        "tc,jcn->jtn",
        normed,
        lax.all_gather(qkv_weight, "seq", axis=2, tiled=True),
        preferred_element_type=jnp.float32,
    ).astype(jnp.bfloat16)
    queries = projected[0].reshape(tok_count, HEADS, HEAD_DIM)
    factor = head_scale / math.sqrt(HEAD_DIM)
    run_max = jnp.full((HEADS, tok_count), -1e30, jnp.float32)
    key_rows = lax.all_gather(projected[1], "seq", axis=0, tiled=True).reshape(-1, HEADS, HEAD_DIM)
    value_rows = lax.all_gather(projected[2], "seq", axis=0, tiled=True).reshape(
        -1, HEADS, HEAD_DIM
    )
    scores = (
        jnp.einsum("thd,nhd->htn", queries, key_rows, preferred_element_type=jnp.float32)
        * factor[:, None, None]
    )
    new_max = jnp.maximum(run_max, jnp.max(scores, axis=2))
    weights = jnp.exp(scores - new_max[:, :, None])
    new_sum = jnp.sum(weights, axis=2)
    new_acc = jnp.einsum(
        "htn,nhd->htd", weights.astype(jnp.bfloat16), value_rows, preferred_element_type=jnp.float32
    )
    heads_out = new_acc / new_sum[:, :, None]
    attended = (
        heads_out.transpose(1, 0, 2).reshape(tok_count, HEADS * HEAD_DIM).astype(jnp.bfloat16)
    )
    base = pooled.astype(jnp.float32)
    return (
        base
        + jnp.dot(
            attended,
            lax.all_gather(out_weight, "seq", axis=1, tiled=True),
            preferred_element_type=jnp.float32,
        )
    ).astype(jnp.bfloat16)


def solution(mesh):
    placed = (
        P(("batch", "seq"), None),
        P(None, None, "seq"),
        P(),
        P(),
        P(None, None, "seq"),
        P(),
        P(None, "seq"),
    )
    return jax.shard_map(
        shards, mesh=mesh, in_specs=placed, out_specs=P(("batch", "seq"), None), check_vma=False
    )
```

profile of v0, /device:TPU:4, one launch (start us, length us, event | category | flops | bytes accessed | tf_op | source)
XLA Modules:
  0.0 799.4 jit_solution(1986249537164564894)
XLA Ops:
  6.5 0.7 all-gather.8.cloned.1.call-update
  7.3 0.7 all-gather.10.cloned.1.call-update
  8.1 1.7 fusion.23
  9.7 3.5 collective-permute-start
  13.2 1.3 collective-permute-start.1
  14.5 248.5 %all-gather.8.cloned.1.call-done = bf16[5,768,1536]{1,2,0:T(8,128)(2,1)} async-done(((bf16[5,768,96]{1,2,0:T(8,128)(2,1)}), bf16[5,768,1536]{1,2,0:T(8,128)(2,1)}) %all-gather.8.cloned.1.call-update) | async-done | bytes 11796496 | tf_op jit(solution)/shard_map/all_gather | solution.py:41
  263.0 3.2 fusion.12
  266.3 3.2 fusion.10
  269.6 1.5 fusion.11
  271.2 1.5 fusion.7
  272.6 1.4 fusion.8
  274.1 1.5 reshape.30
  275.6 5.2 reduce_max.18
  280.9 0.2 convert_reduce_fusion
  281.1 0.3 fusion.15
  281.4 141.0 %all-gather.10.cloned.1.call-done = bf16[3,1536,768]{1,2,0:T(8,128)(2,1)} async-done(((bf16[3,1536,48]{1,2,0:T(8,128)(2,1)}), bf16[3,1536,768]{1,2,0:T(8,128)(2,1)}) %all-gather.10.cloned.1.call-update) | async-done | bytes 7077904 | tf_op jit(solution)/shard_map/all_gather | solution.py:51
  422.4 5.1 fusion.24
  427.6 1.0 fusion.50
  428.6 0.2 all-gather.16.cloned.1.call-start
  428.8 0.3 all-gather.16.cloned.1.call-update
  429.2 0.0 all-gather.12.cloned.1.call-start
  429.2 0.5 all-gather.12.cloned.1.call-update
  429.8 0.2 copy.11
  430.0 139.9 %all-gather.14.cloned.1.call-done = bf16[1,4096,768]{2,1,0:T(8,128)(2,1)} async-done(((bf16[1,256,768]{2,1,0:T(8,128)(2,1)}), bf16[1,4096,768]{2,1,0:T(8,128)(2,1)}) %all-gather.14.cloned.1.call-update) | async-done | bytes 6291472 | tf_op jit(solution)/shard_map/all_gather | solution.py:57
  569.9 8.7 %copy.12 = bf16[1,4096,768]{1,2,0:T(8,128)(2,1)} copy(bf16[1,4096,768]{2,1,0:T(8,128)(2,1)} %all-gather.14.cloned.1.call-done) | data formatting | bytes 12582912 | tf_op jit(solution)/shard_map/all_gather | solution.py:57
  578.6 134.2 %all-gather.16.cloned.1.call-done = bf16[1,4096,768]{2,1,0:T(8,128)(2,1)} async-done(((bf16[1,256,768]{2,1,0:T(8,128)(2,1)}), bf16[1,4096,768]{2,1,0:T(8,128)(2,1)}) %all-gather.16.cloned.1.call-update) | async-done | bytes 6291472 | tf_op jit(solution)/shard_map/all_gather | solution.py:58
  712.8 8.7 %copy.13 = bf16[1,4096,768]{1,2,0:T(8,128)(2,1)} copy(bf16[1,4096,768]{2,1,0:T(8,128)(2,1)} %all-gather.16.cloned.1.call-done) | data formatting | bytes 12582912 | tf_op jit(solution)/shard_map/all_gather | solution.py:58
  721.5 11.1 %multiply_reduce_fusion = (f32[4,256]{1,0:T(4,128)S(1)}, f32[4,256,4096]{2,1,0:T(8,128)}) fusion(f32[4]{0:T(128)S(1)} %broadcast_multiply_fusion.1, bf16[256,4,192]{0,2,1:T(8,128)(2,1)S(1)} %bitcast.41, bf16[4096,4,192]{0,2,1:T(8,128)(2,1)} %bitcast.37), kind=kOutput, calls=%fused_computation.1 | convolution fusion | flops 1619000320 | bytes 23466000 | tf_op jit(solution)/shard_map/thd,nhd->htn/dot_general | solution.py:62
  732.6 8.7 %fusion = f32[4,256]{1,0:T(4,128)S(1)} fusion(f32[4,256,4096]{2,1,0:T(8,128)} %get-tuple-element.11, f32[4,256]{1,0:T(4,128)S(1)} %broadcast_maximum_fusion, f32[4]{0:T(128)S(1)} %broadcast_multiply_fusion.1), kind=kLoop, calls=%fused_computation.2 | loop fusion | flops 12581888 | bytes 16785424 | tf_op jit(solution)/shard_map/reduce_sum | solution.py:67
  741.3 10.8 %fusion.31 = bf16[256,4,192]{0,2,1:T(8,128)(2,1)S(1)} fusion(bf16[4096,4,192]{0,2,1:T(8,128)(2,1)} %bitcast.38, f32[4,256,4096]{2,1,0:T(8,128)} %get-tuple-element.11, f32[4,256]{1,0:T(4,128)S(1)} %broadcast_maximum_fusion, f32[4]{0:T(128)S(1)} %broadcast_multiply_fusion.1, f32[256,4]{0,1:T(4,128)S(1)} %bitcast.42), kind=kOutput, calls=%fused_computation.43 | convolution fusion | flops 1623588864 | bytes 23470096 | tf_op jit(solution)/shard_map/htn,nhd->htd/dot_general | solution.py:68
  752.0 37.5 %all-gather.12.cloned.1.call-done = bf16[768,1536]{0,1:T(8,128)(2,1)} async-done(((bf16[768,96]{0,1:T(8,128)(2,1)}), bf16[768,1536]{0,1:T(8,128)(2,1)}) %all-gather.12.cloned.1.call-update) | async-done | bytes 2359312 | tf_op jit(solution)/shard_map/all_gather | solution.py:80
  789.5 3.4 fusion.9
  (26 shorter events, 0.2 us)
Async XLA Ops:
  6.5 256.5 %all-gather.8.cloned.1.call-start = ((), (), s32[]{:S(2)}) async-start(), calls=%async_computation | async-start | bytes 12533760 | tf_op jit(solution)/shard_map/all_gather | solution.py:41
  7.3 415.2 %all-gather.10.cloned.1.call-start = ((), (), s32[]{:S(2)}) async-start(), calls=%async_computation.1 | async-start | bytes 7520256 | tf_op jit(solution)/shard_map/all_gather | solution.py:51
  8.0 561.9 %all-gather.14.cloned.1.call-start = ((), (), s32[]{:S(2)}) async-start(), calls=%async_computation.3 | async-start | bytes 6684672 | tf_op jit(solution)/shard_map/all_gather | solution.py:57
  9.7 4.8 collective-permute-start
  13.2 253.1 %collective-permute-start.1 = (bf16[2,768]{1,0:T(2,128)(2,1)S(1)}, bf16[2,768]{1,0:T(2,128)(2,1)S(1)}, u32[]{:S(2)}, u32[]{:S(2)}) collective-permute-start(bf16[2,768]{1,0:T(2,128)(2,1)S(1)} %get-tuple-element.9), channel_id=1, source_target_pairs={{1,0},{2,1},{3,2},{4,3},{5,4},{6,5},{7,6},{8,7},{9,8},{10,9},{11,1... | collective-permute-start | bytes 9224 | tf_op jit(solution)/shard_map/ppermute | solution.py:19
  263.0 6.5 slice-start
  263.0 6.5 slice-start.1
  266.3 3.3 slice-start.2
  266.3 3.3 copy-start
  269.6 1.6 copy-start.1
  275.6 146.8 %copy-start.2 = (f32[1536]{0:T(1024)S(1)}, f32[1536]{0:T(1024)}, u32[]{:S(2)}) copy-start(f32[1536]{0:T(1024)} %param.10) | copy-start | bytes 18436
  427.6 2.2 copy-start.3
  428.6 284.2 %all-gather.16.cloned.1.call-start = ((), (), s32[]{:S(2)}) async-start(), calls=%async_computation.4 | async-start | bytes 6684672 | tf_op jit(solution)/shard_map/all_gather | solution.py:58
  429.2 360.3 %all-gather.12.cloned.1.call-start = ((), (), s32[]{:S(2)}) async-start(), calls=%async_computation.2 | async-start | bytes 2506752 | tf_op jit(solution)/shard_map/all_gather | solution.py:80
Sparse Core Ops, SparseCore 0:
  9.1 253.8 all-gather.7
  264.8 157.5 all-gather.9
  428.7 141.1 all-gather.13
  571.5 141.2 all-gather.15
  714.5 74.9 all-gather.11
where the time goes:
time: 800 us; the launch traced here: 799 us
  waiting for transfers between devices  703 us (88%)
  matrix products  41.3 us (5%)
  local copies, waits for them, and re-layouts  20.1 us (3%)
  other arithmetic  16.2 us (2%)
  between operations  13.3 us (2%)
    all_gather x1, waiting for transfers between devices, shards(): lax.all_gather(conv_weight, 'seq', axis=2, tiled=True)  248 us
    all_gather x1, waiting for transfers between devices, shards(): lax.all_gather(qkv_weight, 'seq', axis=2, tiled=True)  141 us
    all_gather x1, waiting for transfers between devices, shards(): lax.all_gather(projected[1], 'seq', axis=0, tiled=True)  140 us
    all_gather x1, waiting for transfers between devices, shards(): lax.all_gather(projected[2], 'seq', axis=0, tiled=True)  134 us
    all_gather x1, waiting for transfers between devices, shards(): lax.all_gather(out_weight, 'seq', axis=1, tiled=True)  37.5 us
  transfers between devices with their start and end apart: 7, of which 5 were waited for; matrix products, arithmetic and copies ran while one was open for 9% of the time, Pallas kernels for 0%

commit v1 on v0

--- a/solution.py
+++ b/solution.py
@@ -48,7 +48,9 @@
     projected = jnp.einsum(
         "tc,jcn->jtn",
         normed,
-        lax.all_gather(qkv_weight, "seq", axis=2, tiled=True),
+        jnp.concatenate(
+            lax.all_to_all(jnp.stack([qkv_weight] * lax.axis_size("seq")), "seq", 0, 0), axis=2
+        ),
         preferred_element_type=jnp.float32,
     ).astype(jnp.bfloat16)
     queries = projected[0].reshape(tok_count, HEADS, HEAD_DIM)

time: 800 us -> 768 us (0.960)
  waiting for transfers between devices: 703 us -> 651 us
  local copies, waits for them, and re-layouts: 20.1 us -> 33.2 us
  starting transfers between devices: 5.11 us -> 15 us
    all_to_all x0 -> x1, waiting for transfers between devices: none -> 207 us  [shards(): lax.all_to_all(jnp.stack([qkv_weight] * lax.axis_size('seq')), 'seq', 0, 0)]
    all_gather x1 -> x0, waiting for transfers between devices: 141 us -> none  [shards(): lax.all_gather(qkv_weight, 'seq', axis=2, tiled=True)]
    all_gather x1, waiting for transfers between devices: 248 us -> 134 us  [shards(): lax.all_gather(conv_weight, 'seq', axis=2, tiled=True)]
    all_to_all x0 -> x1, starting transfers between devices: none -> 9.76 us  [shards(): lax.all_to_all(jnp.stack([qkv_weight] * lax.axis_size('seq')), 'seq', 0, 0)]
  transfers between devices with their start and end apart: 7 -> 7, of which waited for: 5 -> 5; matrix products, arithmetic and copies ran while one was open for 9% -> 8% of each run, Pallas kernels for 0% -> 0%
where the time goes in v1:
time: 768 us; the launch traced here: 767 us
  waiting for transfers between devices  651 us (85%)
  matrix products  39.4 us (5%)
  local copies, waits for them, and re-layouts  33.2 us (4%)
  starting transfers between devices  15 us (2%)
  other arithmetic  15 us (2%)
  between operations  13.3 us (2%)
    all_to_all x1, waiting for transfers between devices, shards(): lax.all_to_all(jnp.stack([qkv_weight] * lax.axis_size('seq')), 'seq', 0, 0)  207 us
    all_gather x1, waiting for transfers between devices, shards(): lax.all_gather(projected[1], 'seq', axis=0, tiled=True)  137 us
    all_gather x1, waiting for transfers between devices, shards(): lax.all_gather(conv_weight, 'seq', axis=2, tiled=True)  134 us
    all_gather x1, waiting for transfers between devices, shards(): lax.all_gather(projected[2], 'seq', axis=0, tiled=True)  134 us
    all_gather x1, waiting for transfers between devices, shards(): lax.all_gather(out_weight, 'seq', axis=1, tiled=True)  37.3 us
  transfers between devices with their start and end apart: 7, of which 5 were waited for; matrix products, arithmetic and copies ran while one was open for 8% of the time, Pallas kernels for 0%

profile of v1, /device:TPU:4, one launch (start us, length us, event | category | flops | bytes accessed | tf_op | source)
XLA Modules:
  0.0 767.3 jit_solution(3775062838968540091)
XLA Ops:
  6.5 0.7 all-gather.7.cloned.1.call-update
  7.3 4.8 stack.2
  12.0 9.8 %all-to-all-start = ((bf16[16,3,1536,48]{2,3,1,0:T(8,128)(2,1)}), bf16[16,3,1536,48]{2,3,1,0:T(8,128)(2,1)}, u32[]{:S(2)}, u32[]{:S(2)}) async-start(bf16[16,3,1536,48]{2,3,1,0:T(8,128)(2,1)} %stack.2), calls=%async_computation | async-start | bytes 14155776 | tf_op jit(solution)/shard_map/all_to_all | solution.py:52
  21.8 0.5 fusion.23
  22.4 3.8 collective-permute-start
  26.2 1.3 collective-permute-start.1
  27.5 206.7 %all-to-all-done = bf16[16,3,1536,48]{2,3,1,0:T(8,128)(2,1)} async-done(((bf16[16,3,1536,48]{2,3,1,0:T(8,128)(2,1)}), bf16[16,3,1536,48]{2,3,1,0:T(8,128)(2,1)}, u32[]{:S(2)}, u32[]{:S(2)}) %all-to-all-start) | async-done | bytes 7077920 | tf_op jit(solution)/shard_map/all_to_all | solution.py:52
  234.2 6.5 copy.16
  240.8 134.4 %all-gather.7.cloned.1.call-done = bf16[5,768,1536]{1,2,0:T(8,128)(2,1)} async-done(((bf16[5,768,96]{1,2,0:T(8,128)(2,1)}), bf16[5,768,1536]{1,2,0:T(8,128)(2,1)}) %all-gather.7.cloned.1.call-update) | async-done | bytes 11796496 | tf_op jit(solution)/shard_map/all_gather | solution.py:41
  375.2 3.4 fusion.11
  378.6 1.7 copy-done
  380.3 1.4 fusion.12
  381.7 1.4 fusion.10
  383.2 1.5 fusion.7
  384.6 1.4 fusion.8
  386.1 1.7 reshape.38
  387.8 5.2 reduce_max.18
  393.0 0.2 convert_reduce_fusion
  393.2 0.3 fusion.15
  393.6 5.1 fusion.24
  398.8 1.0 fusion.50
  399.8 0.7 all-gather.13.cloned.1.call-update
  400.5 0.5 all-gather.9.cloned.1.call-update
  401.3 136.6 %all-gather.11.cloned.1.call-done = bf16[1,4096,768]{2,1,0:T(8,128)(2,1)} async-done(((bf16[1,256,768]{2,1,0:T(8,128)(2,1)}), bf16[1,4096,768]{2,1,0:T(8,128)(2,1)}) %all-gather.11.cloned.1.call-update) | async-done | bytes 6291472 | tf_op jit(solution)/shard_map/all_gather | solution.py:59
  537.9 8.7 %copy.19 = bf16[1,4096,768]{1,2,0:T(8,128)(2,1)} copy(bf16[1,4096,768]{2,1,0:T(8,128)(2,1)} %all-gather.11.cloned.1.call-done) | data formatting | bytes 12582912 | tf_op jit(solution)/shard_map/all_gather | solution.py:59
  546.6 134.4 %all-gather.13.cloned.1.call-done = bf16[1,4096,768]{2,1,0:T(8,128)(2,1)} async-done(((bf16[1,256,768]{2,1,0:T(8,128)(2,1)}), bf16[1,4096,768]{2,1,0:T(8,128)(2,1)}) %all-gather.13.cloned.1.call-update) | async-done | bytes 6291472 | tf_op jit(solution)/shard_map/all_gather | solution.py:60
  681.0 8.6 %copy.20 = bf16[1,4096,768]{1,2,0:T(8,128)(2,1)} copy(bf16[1,4096,768]{2,1,0:T(8,128)(2,1)} %all-gather.13.cloned.1.call-done) | data formatting | bytes 12582912 | tf_op jit(solution)/shard_map/all_gather | solution.py:60
  689.6 11.1 %multiply_reduce_fusion = (f32[4,256]{1,0:T(4,128)S(1)}, f32[4,256,4096]{2,1,0:T(8,128)}) fusion(f32[4]{0:T(128)S(1)} %broadcast_multiply_fusion.1, bf16[256,4,192]{0,2,1:T(8,128)(2,1)S(1)} %bitcast.43, bf16[4096,4,192]{0,2,1:T(8,128)(2,1)} %bitcast.40), kind=kOutput, calls=%fused_computation.1 | convolution fusion | flops 1619000320 | bytes 23466000 | tf_op jit(solution)/shard_map/thd,nhd->htn/dot_general | solution.py:64
  700.6 8.7 %fusion = f32[4,256]{1,0:T(4,128)S(1)} fusion(f32[4,256,4096]{2,1,0:T(8,128)} %get-tuple-element.11, f32[4,256]{1,0:T(4,128)S(1)} %broadcast_maximum_fusion, f32[4]{0:T(128)S(1)} %broadcast_multiply_fusion.1), kind=kLoop, calls=%fused_computation.2 | loop fusion | flops 12581888 | bytes 16785424 | tf_op jit(solution)/shard_map/reduce_sum | solution.py:69
  709.3 10.8 %fusion.31 = bf16[256,4,192]{0,2,1:T(8,128)(2,1)S(1)} fusion(bf16[4096,4,192]{0,2,1:T(8,128)(2,1)} %bitcast.42, f32[4,256,4096]{2,1,0:T(8,128)} %get-tuple-element.11, f32[4,256]{1,0:T(4,128)S(1)} %broadcast_maximum_fusion, f32[4]{0:T(128)S(1)} %broadcast_multiply_fusion.1, f32[256,4]{0,1:T(4,128)S(1)} %bitcast.44), kind=kOutput, calls=%fused_computation.43 | convolution fusion | flops 1623588864 | bytes 23470096 | tf_op jit(solution)/shard_map/htn,nhd->htd/dot_general | solution.py:70
  720.1 37.3 %all-gather.9.cloned.1.call-done = bf16[768,1536]{0,1:T(8,128)(2,1)} async-done(((bf16[768,96]{0,1:T(8,128)(2,1)}), bf16[768,1536]{0,1:T(8,128)(2,1)}) %all-gather.9.cloned.1.call-update) | async-done | bytes 2359312 | tf_op jit(solution)/shard_map/all_gather | solution.py:82
  757.4 3.4 fusion.9
  (22 shorter events, 0.4 us)
Async XLA Ops:
  6.5 368.7 %all-gather.7.cloned.1.call-start = ((), (), s32[]{:S(2)}) async-start(), calls=%async_computation.1 | async-start | bytes 12533760 | tf_op jit(solution)/shard_map/all_gather | solution.py:41
  12.0 9.8 %copy-start.1 = (bf16[512,768]{1,0:T(8,128)(2,1)S(1)}, bf16[512,768]{1,0:T(8,128)(2,1)}, u32[]{:S(2)}) copy-start(bf16[512,768]{1,0:T(8,128)(2,1)} %param.7) | copy-start | bytes 2359300
  12.0 222.2 %all-to-all-start = ((bf16[16,3,1536,48]{2,3,1,0:T(8,128)(2,1)}), bf16[16,3,1536,48]{2,3,1,0:T(8,128)(2,1)}, u32[]{:S(2)}, u32[]{:S(2)}) async-start(bf16[16,3,1536,48]{2,3,1,0:T(8,128)(2,1)} %stack.2), calls=%async_computation | async-start | bytes 14155776 | tf_op jit(solution)/shard_map/all_to_all | solution.py:52
  21.8 516.1 %all-gather.11.cloned.1.call-start = ((), (), s32[]{:S(2)}) async-start(), calls=%async_computation.3 | async-start | bytes 6684672 | tf_op jit(solution)/shard_map/all_gather | solution.py:59
  22.4 356.1 %collective-permute-start = (bf16[2,768]{1,0:T(2,128)(2,1)S(1)}, bf16[2,768]{1,0:T(2,128)(2,1)S(1)}, u32[]{:S(2)}, u32[]{:S(2)}) collective-permute-start(bf16[2,768]{1,0:T(2,128)(2,1)S(1)} %get-tuple-element.8), channel_id=1, source_target_pairs={{0,1},{1,2},{2,3},{3,4},{4,5},{5,6},{6,7},{7,8},{8,9},{9,10},{10,1... | collective-permute-start | bytes 9224 | tf_op jit(solution)/shard_map/ppermute | solution.py:16
  26.2 355.5 %collective-permute-start.1 = (bf16[2,768]{1,0:T(2,128)(2,1)S(1)}, bf16[2,768]{1,0:T(2,128)(2,1)S(1)}, u32[]{:S(2)}, u32[]{:S(2)}) collective-permute-start(bf16[2,768]{1,0:T(2,128)(2,1)S(1)} %get-tuple-element.9), channel_id=1, source_target_pairs={{1,0},{2,1},{3,2},{4,3},{5,4},{6,5},{7,6},{8,7},{9,8},{10,9},{11,1... | collective-permute-start | bytes 9224 | tf_op jit(solution)/shard_map/ppermute | solution.py:19
  375.2 5.1 copy-start
  381.7 1.5 copy-start.2
  387.8 5.8 copy-start.3
  398.7 2.3 copy-start.4
  399.8 281.2 %all-gather.13.cloned.1.call-start = ((), (), s32[]{:S(2)}) async-start(), calls=%async_computation.4 | async-start | bytes 6684672 | tf_op jit(solution)/shard_map/all_gather | solution.py:60
  400.5 356.9 %all-gather.9.cloned.1.call-start = ((), (), s32[]{:S(2)}) async-start(), calls=%async_computation.2 | async-start | bytes 2506752 | tf_op jit(solution)/shard_map/all_gather | solution.py:82
Sparse Core Ops, SparseCore 0:
  9.1 365.9 all-gather.6
  399.9 137.9 all-gather.10
  539.7 141.2 all-gather.12
  682.6 74.6 all-gather.8
